TPU v7x, 32 devices: a whole 2x2x4 slice. The times are simulated.
32 devices in a mesh: rep: 16 (over z, y, core), fsdp: 2 (over x).
Axes of the slice: x: 2, y: 2, z: 4, core: 2. Of those that a mesh axis runs over, the one named last changes fastest.
Arguments:
- tokens: bfloat16 [256, 197, 384], P(('rep', 'fsdp')), may hold values from -6 to 6
- gain_one: bfloat16 [384], P('fsdp'), may hold values from 0.25 to 1.75
- shift_one: bfloat16 [384], P('fsdp'), may hold values from -1.75 to 1.75
- qkv_weight: bfloat16 [384, 1152], P('fsdp'), may hold values from -0.3125 to 0.3125
- query_bias: bfloat16 [384], P('fsdp'), may hold values from -3 to 3
- value_bias: bfloat16 [384], P('fsdp'), may hold values from -3 to 3
- out_weight: bfloat16 [384, 384], P('fsdp'), may hold values from -1.25 to 1.25
- out_bias: bfloat16 [384], P('fsdp'), may hold values from -1.75 to 1.75
- gain_two: bfloat16 [384], P('fsdp'), may hold values from 0.25 to 1.75
- shift_two: bfloat16 [384], P('fsdp'), may hold values from -1.75 to 1.75
- lift_weight: bfloat16 [384, 1536], P('fsdp'), may hold values from -0.3125 to 0.3125
- lift_bias: bfloat16 [1536], P('fsdp'), may hold values from -3 to 3
- drop_weight: bfloat16 [1536, 384], P('fsdp'), may hold values from -0.15625 to 0.15625
- drop_bias: bfloat16 [384], P('fsdp'), may hold values from -1.75 to 1.75
- cotangent: bfloat16 [256, 197, 384], P(('rep', 'fsdp')), may hold values from -12 to 12
Outputs:
- output: bfloat16 [256, 197, 384], P(('rep', 'fsdp'))
- input_grad: bfloat16 [256, 197, 384], P(('rep', 'fsdp'))
- grad_gain_one: float32 [384], P('fsdp')
- grad_shift_one: float32 [384], P('fsdp')
- grad_qkv_weight: float32 [384, 1152], P('fsdp')
- grad_query_bias: float32 [384], P('fsdp')
- grad_value_bias: float32 [384], P('fsdp')
- grad_out_weight: float32 [384, 384], P('fsdp')
- grad_out_bias: float32 [384], P('fsdp')
- grad_gain_two: float32 [384], P('fsdp')
- grad_shift_two: float32 [384], P('fsdp')
- grad_lift_weight: float32 [384, 1536], P('fsdp')
- grad_lift_bias: float32 [1536], P('fsdp')
- grad_drop_weight: float32 [1536, 384], P('fsdp')
- grad_drop_bias: float32 [384], P('fsdp')
All inputs are finite; a program needn't handle non-finite values.
Results may differ from a plain program's by a relative error of at most 0.023.
Values may be sent and summed in bfloat16 or wider, within the bound.
No kernel may reach another device: no remote copies, remote signals or barrier semaphores. Data moves between devices by JAX's collectives and lax.ppermute only.
A program may use at most 128 MiB of HBM per device.

v0:
```python
import jax
import jax.numpy as jnp
from jax import lax
from jax.sharding import PartitionSpec as P

HEADS = 6
HEAD_DIM = 64
epsilon = 1e-06
root_half = 0.7071067811865476
gauss_norm = 0.3989422804014327


def norm_forward(inputs, gain_vec, shift_vec):
    average = jnp.mean(inputs, axis=-1, keepdims=True)
    centred = inputs - average
    variance = jnp.mean(centred * centred, axis=-1, keepdims=True)
    inverse = lax.rsqrt(variance + epsilon)
    normal = centred * inverse
    return (normal * gain_vec + shift_vec, normal, inverse)


def norm_backward(grad_out, normal, inverse, gain_vec):
    grad_gain = jnp.sum(grad_out * normal, axis=0)
    grad_shift = jnp.sum(grad_out, axis=0)
    scaled = grad_out * gain_vec
    grad_in = inverse * (
        scaled
        - jnp.mean(scaled, axis=-1, keepdims=True)
        - normal * jnp.mean(scaled * normal, axis=-1, keepdims=True)
    )
    return (grad_in, grad_gain, grad_shift)


def product(left, right):
    return jnp.dot(left, right, preferred_element_type=jnp.float32)


def product_left(left, right):
    return lax.dot_general(
        left, right, (((0,), (0,)), ((), ())), preferred_element_type=jnp.float32
    )


def product_right(left, right):
    return lax.dot_general(
        left, right, (((1,), (1,)), ((), ())), preferred_element_type=jnp.float32
    )


def raw_scores(query_part, key_part):
    scale_factor = query_part.shape[-1] ** (-0.5)
    return (
        jnp.einsum("iqhe,ikhe->ihqk", query_part, key_part, preferred_element_type=jnp.float32)
        * scale_factor
    )


def per_device(
    tokens,
    gain_one,
    shift_one,
    qkv_weight,
    query_bias,
    value_bias,
    out_weight,
    out_bias,
    gain_two,
    shift_two,
    lift_weight,
    lift_bias,
    drop_weight,
    drop_bias,
    cotangent,
):
    gathered = (
        lax.all_gather(gain_one, "fsdp", axis=0, tiled=True),
        lax.all_gather(shift_one, "fsdp", axis=0, tiled=True),
        lax.all_gather(qkv_weight, "fsdp", axis=0, tiled=True),
        lax.all_gather(query_bias, "fsdp", axis=0, tiled=True),
        lax.all_gather(value_bias, "fsdp", axis=0, tiled=True),
        lax.all_gather(out_weight, "fsdp", axis=0, tiled=True),
        lax.all_gather(out_bias, "fsdp", axis=0, tiled=True),
        lax.all_gather(gain_two, "fsdp", axis=0, tiled=True),
        lax.all_gather(shift_two, "fsdp", axis=0, tiled=True),
        lax.all_gather(lift_weight, "fsdp", axis=0, tiled=True),
        lax.all_gather(lift_bias, "fsdp", axis=0, tiled=True),
        lax.all_gather(drop_weight, "fsdp", axis=0, tiled=True),
        lax.all_gather(drop_bias, "fsdp", axis=0, tiled=True),
    )
    (
        full_gain_one,
        full_shift_one,
        full_qkv,
        full_query_bias,
        full_value_bias,
        full_out,
        full_out_bias,
        full_gain_two,
        full_shift_two,
        full_lift,
        full_lift_bias,
        full_drop,
        full_drop_bias,
    ) = gathered
    images, length, width = tokens.shape
    tok_rows = images * length
    scale_factor = HEAD_DIM ** (-0.5)
    flat_in = tokens.astype(jnp.float32).reshape(tok_rows, width)
    normed_f, normal_one, inverse_one = norm_forward(
        flat_in, full_gain_one.astype(jnp.float32), full_shift_one.astype(jnp.float32)
    )
    normed = normed_f.astype(jnp.bfloat16)
    qkv_bias = jnp.concatenate(
        [full_query_bias, jnp.zeros_like(full_query_bias), full_value_bias]
    ).astype(jnp.float32)
    projected = (product(normed, full_qkv) + qkv_bias).astype(jnp.bfloat16)
    split_heads = projected.reshape(images, length, 3, HEADS, HEAD_DIM)
    query_part = split_heads[:, :, 0]
    key_part = split_heads[:, :, 1]
    value_part = split_heads[:, :, 2]
    scores = raw_scores(query_part, key_part)
    top_score = jnp.max(scores, axis=-1, keepdims=True)
    log_total = top_score + jnp.log(jnp.sum(jnp.exp(scores - top_score), axis=-1, keepdims=True))
    soft_weights = jnp.exp(scores - log_total).astype(jnp.bfloat16)
    mixed = (
        jnp.einsum("ihqk,ikhe->iqhe", soft_weights, value_part, preferred_element_type=jnp.float32)
        .reshape(tok_rows, width)
        .astype(jnp.bfloat16)
    )
    middle = flat_in + product(mixed, full_out) + full_out_bias.astype(jnp.float32)
    normed_two_f, normal_two, inverse_two = norm_forward(
        middle, full_gain_two.astype(jnp.float32), full_shift_two.astype(jnp.float32)
    )
    normed_two = normed_two_f.astype(jnp.bfloat16)
    hidden = product(normed_two, full_lift) + full_lift_bias.astype(jnp.float32)
    active = jax.nn.gelu(hidden, approximate=False).astype(jnp.bfloat16)
    result = middle + product(active, full_drop) + full_drop_bias.astype(jnp.float32)
    output = result.astype(jnp.bfloat16).reshape(tokens.shape)
    back_gain_one, back_qkv, back_out, back_gain_two, back_lift, back_drop = (
        lax.all_gather(gain_one, "fsdp", axis=0, tiled=True),
        lax.all_gather(qkv_weight, "fsdp", axis=0, tiled=True),
        lax.all_gather(out_weight, "fsdp", axis=0, tiled=True),
        lax.all_gather(gain_two, "fsdp", axis=0, tiled=True),
        lax.all_gather(lift_weight, "fsdp", axis=0, tiled=True),
        lax.all_gather(drop_weight, "fsdp", axis=0, tiled=True),
    )
    grad_flat = cotangent.reshape(tok_rows, width)
    grad_outer = grad_flat.astype(jnp.float32)
    grad_drop_weight = product_left(active, grad_flat)
    grad_drop_bias = jnp.sum(grad_outer, axis=0)
    d_active = product_right(grad_flat, back_drop)
    slope = (
        0.5 * (1.0 + lax.erf(hidden * root_half))
        + hidden * jnp.exp(-0.5 * hidden * hidden) * gauss_norm
    )
    d_hidden = (d_active * slope).astype(jnp.bfloat16)
    grad_lift_weight = product_left(normed_two, d_hidden)
    grad_lift_bias = jnp.sum(d_hidden.astype(jnp.float32), axis=0)
    d_normed_two = product_right(d_hidden, back_lift)
    d_from_norm, grad_gain_two, grad_shift_two = norm_backward(
        d_normed_two, normal_two, inverse_two, back_gain_two.astype(jnp.float32)
    )
    d_middle = grad_outer + d_from_norm
    d_attended = d_middle.astype(jnp.bfloat16)
    grad_out_weight = product_left(mixed, d_attended)
    grad_out_bias = jnp.sum(d_attended.astype(jnp.float32), axis=0)
    d_mixed = (
        product_right(d_attended, back_out)
        .astype(jnp.bfloat16)
        .reshape(images, length, HEADS, HEAD_DIM)
    )
    again_probs = jnp.exp(raw_scores(query_part, key_part) - log_total)
    again_soft = again_probs.astype(jnp.bfloat16)
    d_value = jnp.einsum("ihqk,iqhe->ikhe", again_soft, d_mixed, preferred_element_type=jnp.float32)
    d_probs = jnp.einsum("iqhe,ikhe->ihqk", d_mixed, value_part, preferred_element_type=jnp.float32)
    row_delta = jnp.sum(again_probs * d_probs, axis=-1, keepdims=True)
    d_scores = (again_probs * (d_probs - row_delta)).astype(jnp.bfloat16)
    d_query = (
        jnp.einsum("ihqk,ikhe->iqhe", d_scores, key_part, preferred_element_type=jnp.float32)
        * scale_factor
    )
    d_key = (
        jnp.einsum("ihqk,iqhe->ikhe", d_scores, query_part, preferred_element_type=jnp.float32)
        * scale_factor
    )
    d_projected = (
        jnp.stack([d_query, d_key, d_value], axis=2)
        .reshape(tok_rows, 3 * width)
        .astype(jnp.bfloat16)
    )
    grad_qkv_weight = product_left(normed, d_projected)
    column_sums = jnp.sum(d_projected.astype(jnp.float32), axis=0)
    grad_query_bias = column_sums[:width]
    grad_value_bias = column_sums[2 * width :]
    d_normed = product_right(d_projected, back_qkv)
    d_first, grad_gain_one, grad_shift_one = norm_backward(
        d_normed, normal_one, inverse_one, back_gain_one.astype(jnp.float32)
    )
    input_grad = (d_middle + d_first).astype(jnp.bfloat16).reshape(tokens.shape)
    owned = (
        lax.psum_scatter(
            grad_gain_one.astype(jnp.bfloat16), "fsdp", scatter_dimension=0, tiled=True
        ).astype(jnp.float32),
        lax.psum_scatter(
            grad_shift_one.astype(jnp.bfloat16), "fsdp", scatter_dimension=0, tiled=True
        ).astype(jnp.float32),
        lax.psum_scatter(
            grad_qkv_weight.astype(jnp.bfloat16), "fsdp", scatter_dimension=0, tiled=True
        ).astype(jnp.float32),
        lax.psum_scatter(
            grad_query_bias.astype(jnp.bfloat16), "fsdp", scatter_dimension=0, tiled=True
        ).astype(jnp.float32),
        lax.psum_scatter(
            grad_value_bias.astype(jnp.bfloat16), "fsdp", scatter_dimension=0, tiled=True
        ).astype(jnp.float32),
        lax.psum_scatter(
            grad_out_weight.astype(jnp.bfloat16), "fsdp", scatter_dimension=0, tiled=True
        ).astype(jnp.float32),
        lax.psum_scatter(
            grad_out_bias.astype(jnp.bfloat16), "fsdp", scatter_dimension=0, tiled=True
        ).astype(jnp.float32),
        lax.psum_scatter(
            grad_gain_two.astype(jnp.bfloat16), "fsdp", scatter_dimension=0, tiled=True
        ).astype(jnp.float32),
        lax.psum_scatter(
            grad_shift_two.astype(jnp.bfloat16), "fsdp", scatter_dimension=0, tiled=True
        ).astype(jnp.float32),
        lax.psum_scatter(
            grad_lift_weight.astype(jnp.bfloat16), "fsdp", scatter_dimension=0, tiled=True
        ).astype(jnp.float32),
        lax.psum_scatter(
            grad_lift_bias.astype(jnp.bfloat16), "fsdp", scatter_dimension=0, tiled=True
        ).astype(jnp.float32),
        lax.psum_scatter(
            grad_drop_weight.astype(jnp.bfloat16), "fsdp", scatter_dimension=0, tiled=True
        ).astype(jnp.float32),
        lax.psum_scatter(
            grad_drop_bias.astype(jnp.bfloat16), "fsdp", scatter_dimension=0, tiled=True
        ).astype(jnp.float32),
    )
    final = (
        lax.psum(owned[0].astype(jnp.bfloat16), "rep").astype(jnp.float32),
        lax.psum(owned[1].astype(jnp.bfloat16), "rep").astype(jnp.float32),
        lax.psum(owned[2].astype(jnp.bfloat16), "rep").astype(jnp.float32),
        lax.psum(owned[3].astype(jnp.bfloat16), "rep").astype(jnp.float32),
        lax.psum(owned[4].astype(jnp.bfloat16), "rep").astype(jnp.float32),
        lax.psum(owned[5].astype(jnp.bfloat16), "rep").astype(jnp.float32),
        lax.psum(owned[6].astype(jnp.bfloat16), "rep").astype(jnp.float32),
        lax.psum(owned[7].astype(jnp.bfloat16), "rep").astype(jnp.float32),
        lax.psum(owned[8].astype(jnp.bfloat16), "rep").astype(jnp.float32),
        lax.psum(owned[9].astype(jnp.bfloat16), "rep").astype(jnp.float32),
        lax.psum(owned[10].astype(jnp.bfloat16), "rep").astype(jnp.float32),
        lax.psum(owned[11].astype(jnp.bfloat16), "rep").astype(jnp.float32),
        lax.psum(owned[12].astype(jnp.bfloat16), "rep").astype(jnp.float32),
    )
    return (output, input_grad) + tuple(final)


def solution(mesh):
    in_specs = (
        P(("rep", "fsdp"), None, None),
        P("fsdp"),
        P("fsdp"),
        P("fsdp", None),
        P("fsdp"),
        P("fsdp"),
        P("fsdp", None),
        P("fsdp"),
        P("fsdp"),
        P("fsdp"),
        P("fsdp", None),
        P("fsdp"),
        P("fsdp", None),
        P("fsdp"),
        P(("rep", "fsdp"), None, None),
    )
    out_specs = (
        P(("rep", "fsdp"), None, None),
        P(("rep", "fsdp"), None, None),
        P("fsdp"),
        P("fsdp"),
        P("fsdp", None),
        P("fsdp"),
        P("fsdp"),
        P("fsdp", None),
        P("fsdp"),
        P("fsdp"),
        P("fsdp"),
        P("fsdp", None),
        P("fsdp"),
        P("fsdp", None),
        P("fsdp"),
    )
    return jax.shard_map(
        per_device, mesh=mesh, in_specs=in_specs, out_specs=out_specs, check_vma=False
    )
```

profile of v0, /device:TPU:0, one launch (start us, length us, event | category | flops | bytes accessed | tf_op | source)
XLA Modules:
  0.0 416.0 jit_solution(2073940774700629270)
XLA Ops:
  16.4 5.9 %all-reduce.20 = (bf16[384]{0:T(512)(128)(2,1)S(1)}, bf16[384]{0:T(512)(128)(2,1)S(1)}, bf16[384]{0:T(512)(128)(2,1)S(1)}, bf16[384]{0:T(512)(128)(2,1)S(1)}, bf...) all-reduce(bf16[384]{0:T(512)(128)(2,1)S(1)} %dynamic-update-slice., ...), channel_id=1, replica_groups=mesh['rep'=16,'fsdp'=2] {'fsdp'}, use_global_device_ids=true, to_apply=%add.3 | all-reduce | flops 2688 | bytes 10752
  24.4 20.0 %all_gather.47 = bf16[384,1152]{1,0:T(8,128)(2,1)S(1)} all-gather(bf16[192,1152]{1,0:T(8,128)(2,1)S(1)} %copy-done.15), channel_id=1, replica_groups=mesh['rep'=16,'fsdp'=2] {'fsdp'}, dimensions={0}, use_global_device_ids=true | all-gather | bytes 1327104 | tf_op jit(solution)/shard_map/all_gather | solution.py:78
  45.3 4.2 %fusion.16 = bf16[1576,1152]{1,0:T(8,128)(2,1)} fusion(bf16[384,1152]{1,0:T(8,128)(2,1)S(1)} %all_gather.47, f32[1152]{0:T(1024)S(1)} %maximum_convert_fusion.1, f32[1576,384]{1,0:T(8,128)S(1)} %reshape.179, f32[384]{0:T(512)S(1)} %convert_element_type.206, f32[384]{0:T(512)S(1)} %convert_element_type.205, f32[1576]{0:T(1024)S(1)} %rsqrt.21, f32[1576]{0:T(1024)S(1)} %div.27), kind=kOutput, calls=%fused_computation.34 | convolution fusion | flops 1401000960 | bytes 6956864 | tf_op jit(solution)/shard_map/dot_general | solution.py:35
  49.5 11.8 %reshape.237 = bf16[8,197,3,6,64]{4,3,2,1,0:T(8,128)(2,1)} reshape(bf16[1576,1152]{1,0:T(8,128)(2,1)} %fusion.16) | data formatting | bytes 7262208 | tf_op jit(solution)/shard_map/reshape | solution.py:117
  61.2 6.7 %fusion.43 = (bf16[8,197,1,6,64]{4,3,2,1,0:T(8,128)(2,1)}, bf16[8,197,1,6,64]{4,3,2,1,0:T(8,128)(2,1)}, bf16[8,197,1,6,64]{4,3,2,1,0:T(8,128)(2,1)}) fusion(bf16[8,197,3,6,64]{4,3,2,1,0:T(8,128)(2,1)} %reshape.237), kind=kLoop, calls=%fused_computation.96 | loop fusion | bytes 7262208 | tf_op jit(solution)/shard_map/slice | solution.py:118
  67.9 3.5 copy.114
  71.4 4.0 copy.115
  80.8 3.5 copy.113
  84.3 6.3 %fusion.29 = bf16[8,197,6,64]{1,3,2,0:T(8,128)(2,1)S(1)} fusion(bf16[8,197,1,6,64]{1,4,3,0,2:T(8,128)(2,1)S(1)} %copy.113, f32[8,6,197,197]{2,3,1,0:T(8,128)} %copy-done, f32[8,6,197]{2,1,0:T(8,128)S(1)} %log_add_fusion), kind=kOutput, calls=%fused_computation.73 | convolution fusion | flops 244636176 | bytes 9909888 | tf_op jit(solution)/shard_map/ihqk,ikhe->iqhe/dot_general | solution.py:126
  94.2 6.2 %all_gather.50 = bf16[384,384]{1,0:T(8,128)(2,1)S(1)} all-gather(bf16[192,384]{1,0:T(8,128)(2,1)S(1)} %copy-done.17), channel_id=1, replica_groups=mesh['rep'=16,'fsdp'=2] {'fsdp'}, dimensions={0}, use_global_device_ids=true | all-gather | bytes 442368 | tf_op jit(solution)/shard_map/all_gather | solution.py:81
  104.3 4.3 %all-gather = bf16[2,1,768]{2,1,0:T(2,128)(2,1)S(1)} all-gather(bf16[1,1,768]{2,1,0:T(2,128)(2,1)S(1)} %reshape.209), channel_id=1, replica_groups=mesh['rep'=16,'fsdp'=2] {'fsdp'}, dimensions={0}, use_global_device_ids=true | all-gather | bytes 4608 | tf_op jit(solution)/shard_map/all_gather | solution.py:86
  119.7 26.4 %fusion.2 = (bf16[1576,1536]{1,0:T(8,128)(2,1)}, f32[1576,1536]{1,0:T(8,128)}) fusion(f32[1536]{0:T(1024)S(1)} %reshape.211, bf16[384,1536]{1,0:T(8,128)(2,1)} %all-gather.4.cloned.1.call-done, f32[1576,384]{1,0:T(8,128)S(1)} %get-tuple-element.127, f32[384]{0:T(512)S(1)} %convert_element_type.216, f32[384]{0:T(512)S(1)} %convert_element_type.215, ...), kind=kOutput, calls=%fused_computation.9 | convolution fusion | flops 2021919744 | bytes 18146624 | tf_op jit(solution)/shard_map/dot_general | solution.py:35
  146.0 8.6 %fusion.47 = (bf16[1536]{0:T(1024)(128)(2,1)S(1)}, bf16[1576,1536]{1,0:T(8,128)(2,1)S(1)}) fusion(f32[1576,1536]{1,0:T(8,128)} %get-tuple-element.129, bf16[1576,384]{1,0:T(8,128)(2,1)} %reshape.182, bf16[1536,384]{1,0:T(8,128)(2,1)} %all-gather.6.cloned.1.call-done), kind=kOutput, calls=%fused_computation.100 | convolution fusion | flops 1885751808 | bytes 16917504 | tf_op jit(solution)/shard_map/dot_general | solution.py:45
  154.7 3.3 multiply_reduce_fusion.2
  164.9 4.8 %reshape.238 = bf16[8,197,6,64]{3,2,1,0:T(8,128)(2,1)} reshape(bf16[1576,384]{1,0:T(8,128)(2,1)} %convolution_convert_fusion.3) | data formatting | bytes 2420736 | tf_op jit(solution)/shard_map/reshape | solution.py:170
  169.6 5.0 %copy.95 = bf16[8,197,6,64]{1,3,2,0:T(8,128)(2,1)} copy(bf16[8,197,6,64]{3,2,1,0:T(8,128)(2,1)} %reshape.238) | data formatting | bytes 2420736 | tf_op jit(solution)/shard_map/reshape | solution.py:170
  174.6 11.1 %multiply_reduce_fusion = (f32[8,6,197]{2,1,0:T(8,128)S(1)}, f32[8,6,197,197]{2,3,1,0:T(8,128)}) fusion(f32[8,6,197,197]{2,3,1,0:T(8,128)} %copy-done, f32[8,6,197]{2,1,0:T(8,128)S(1)} %log_add_fusion, bf16[8,197,6,64]{1,3,2,0:T(8,128)(2,1)} %copy.95, bf16[8,197,1,6,64]{1,4,3,0,2:T(8,128)(2,1)} %copy-done.7), kind=kOutput, calls=%fused_computation.3 | convolution fusion | flops 245884368 | bytes 17399040 | tf_op jit(solution)/shard_map/iqhe,ikhe->ihqk/dot_general | solution.py:175
  185.7 11.5 %multiply_convert_fusion = bf16[8,6,197,197]{2,3,1,0:T(8,128)(2,1)} fusion(f32[8,6,197,197]{2,3,1,0:T(8,128)} %get-tuple-element.132, f32[8,6,197,197]{2,3,1,0:T(8,128)} %copy-done, f32[8,6,197]{2,1,0:T(8,128)S(1)} %get-tuple-element.131, f32[8,6,197]{2,1,0:T(8,128)S(1)} %log_add_fusion), kind=kLoop, calls=%fused_computation.2 | loop fusion | flops 9314160 | bytes 18703968 | tf_op jit(solution)/shard_map/convert_element_type | solution.py:177
  197.2 5.2 %multiply_bitcast_fusion.1 = bf16[8,197,1,6,64]{1,4,3,0,2:T(8,128)(2,1)} fusion(bf16[8,6,197,197]{2,3,1,0:T(8,128)(2,1)} %multiply_convert_fusion, bf16[8,197,1,6,64]{1,4,3,0,2:T(8,128)(2,1)} %copy-done.1), kind=kOutput, calls=%fused_computation.37 | convolution fusion | flops 239652864 | bytes 6146400 | tf_op jit(solution)/shard_map/ihqk,ikhe->iqhe/dot_general | solution.py:179
  202.4 5.4 %multiply_bitcast_fusion = bf16[8,197,1,6,64]{1,4,3,0,2:T(8,128)(2,1)} fusion(bf16[8,6,197,197]{2,3,1,0:T(8,128)(2,1)} %multiply_convert_fusion, bf16[8,197,1,6,64]{1,4,3,0,2:T(8,128)(2,1)S(1)} %copy-done.10), kind=kOutput, calls=%fused_computation.36 | convolution fusion | flops 239652864 | bytes 6146400 | tf_op jit(solution)/shard_map/ihqk,iqhe->ikhe/dot_general | solution.py:183
  214.2 5.5 %copy.100 = bf16[8,197,3,6,64]{1,0,4,3,2:T(8,128)(2,1)} copy(bf16[8,197,3,6,64]{1,4,3,0,2:T(8,128)(2,1)S(1)} %get-tuple-element.116) | data formatting | bytes 7262208 | tf_op jit(solution)/shard_map/convert_element_type | solution.py:189
  219.6 8.9 %convert_element_type.228 = bf16[1576,1152]{0,1:T(8,128)(2,1)} reshape(bf16[8,197,3,6,64]{1,0,4,3,2:T(8,128)(2,1)} %copy.100) | data formatting | bytes 7262208 | tf_op jit(solution)/shard_map/convert_element_type | solution.py:189
  228.5 5.4 %convolution_convert_fusion = bf16[384,1152]{1,0:T(8,128)(2,1)} fusion(bf16[1576,384]{1,0:T(8,128)(2,1)} %convert_element_type.235, bf16[1576,1152]{0,1:T(8,128)(2,1)} %convert_element_type.228), kind=kOutput, calls=%fused_computation.42 | convolution fusion | flops 1394786304 | bytes 5726208 | tf_op jit(solution)/shard_map/dot_general | solution.py:39
  233.9 6.6 %convolution_convert_fusion.2 = bf16[384,1536]{1,0:T(8,128)(2,1)} fusion(bf16[1576,1536]{1,0:T(8,128)(2,1)} %copy-done.37, f32[1576,384]{1,0:T(8,128)} %copy-done.2, f32[384]{0:T(512)S(1)} %convert_element_type.216, f32[384]{0:T(512)S(1)} %convert_element_type.215, f32[1576]{0:T(1024)S(1)} %add_rsqrt_fusion, f32[1576]{0:T(1024)S(1)} %broadcast_multiply_fusion.4), kind=kOutput, calls=%fused_computation.45 | convolution fusion | flops 1862740992 | bytes 8457536 | tf_op jit(solution)/shard_map/dot_general | solution.py:39
  240.7 6.8 %convolution_convert_fusion.1 = bf16[1536,384]{1,0:T(8,128)(2,1)} fusion(bf16[1576,1536]{1,0:T(8,128)(2,1)} %get-tuple-element.128, bf16[1576,384]{1,0:T(8,128)(2,1)} %reshape.182), kind=kOutput, calls=%fused_computation.44 | convolution fusion | flops 1859715072 | bytes 7231488 | tf_op jit(solution)/shard_map/dot_general | solution.py:39
  250.9 6.4 %multiply_reduce_fusion.3 = (bf16[384]{0:T(512)(128)(2,1)S(1)}, f32[1576]{0:T(1024)S(1)}, f32[1576]{0:T(1024)S(1)}, bf16[384]{0:T(512)(128)(2,1)S(1)}, f32[1576,384]{1,0:T(8,128)S(1)}) fusion(f32[1576,384]{1,0:T(8,128)} %copy-done.4, f32[1576]{0:T(1024)S(1)} %copy-done.22, f32[1576]{0:T(1024)S(1)} %copy-done.20, f32[384]{0:T(512)S(1)} %copy-done.24, ...), kind=kOutput, calls=%fused_computation.49 | convolution fusion | flops 1399786752 | bytes 9385600 | tf_op jit(solution)/shard_map/dot_general | solution.py:45
  259.6 17.5 %reduce-scatter.9.cloned.1.call-done = bf16[192,1536]{1,0:T(8,128)(2,1)} async-done(((bf16[384,1536]{1,0:T(8,128)(2,1)}), bf16[192,1536]{1,0:T(8,128)(2,1)}) %reduce-scatter.9.cloned.1.call-update) | async-done | bytes 589840 | tf_op jit(solution)/shard_map/reduce_scatter | solution.py:228
  277.1 24.5 %reduce-scatter.11.cloned.1.call-done = bf16[768,384]{1,0:T(8,128)(2,1)} async-done(((bf16[1536,384]{1,0:T(8,128)(2,1)}), bf16[768,384]{1,0:T(8,128)(2,1)}) %reduce-scatter.11.cloned.1.call-update) | async-done | bytes 589840 | tf_op jit(solution)/shard_map/reduce_scatter | solution.py:234
  301.8 7.0 %all-reduce.19 = (bf16[384]{0:T(512)(128)(2,1)S(1)}, bf16[384]{0:T(512)(128)(2,1)S(1)}, bf16[384]{0:T(512)(128)(2,1)S(1)}, bf16[384]{0:T(512)(128)(2,1)S(1)}, bf...) all-reduce(bf16[384]{0:T(512)(128)(2,1)S(1)} %dynamic-update-slice., ...), channel_id=1, replica_groups=mesh['rep'=16,'fsdp'=2] {'fsdp'}, use_global_device_ids=true, to_apply=%add.7 | all-reduce | flops 4992 | bytes 19968
  309.5 32.4 %all-reduce.17 = (bf16[192]{0:T(256)(128)(2,1)S(1)}, bf16[192]{0:T(256)(128)(2,1)S(1)}, bf16[192]{0:T(256)(128)(2,1)S(1)}, bf16[192]{0:T(256)(128)(2,1)S(1)}, bf...) all-reduce(bf16[192]{0:T(256)(128)(2,1)S(1)} %dynamic-slice.9, ...), channel_id=1, replica_groups=mesh['rep'=16,'fsdp'=2] {'rep'}, use_global_device_ids=true, to_apply=%region_13.0 | all-reduce | flops 2304 | bytes 9216 | tf_op jit(solution)/shard_map/psum | solution.py:242
  352.4 6.1 %fusion.20 = bf16[1576,384]{1,0:T(8,128)(2,1)} fusion(f32[1576,384]{1,0:T(8,128)S(1)} %copy-done.3, bf16[1576,1536]{1,0:T(8,128)(2,1)} %get-tuple-element.128, bf16[1536,384]{1,0:T(8,128)(2,1)S(1)} %copy-done.27, f32[384]{0:T(512)S(1)} %convert_element_type.220), kind=kOutput, calls=%fused_computation.43 | convolution fusion | flops 1860940800 | bytes 9653760 | tf_op jit(solution)/shard_map/dot_general | solution.py:35
  361.4 41.4 %all-reduce.23.cloned.1.call-done = (bf16[192,1152]{1,0:T(8,128)(2,1)}, bf16[192,384]{1,0:T(8,128)(2,1)}, bf16[192,1536]{1,0:T(8,128)(2,1)}, bf16[768,384]{1,0:T(8,128)(2,1)}) async-done(((bf16[192,1152]{1,0:T(8,128)(2,1)}, bf16[192,384]{1,0:T(8,128)(2,1)}, bf16[192,1536]{1,0:T(8,128)(2,1)}, bf16[768,384]{1,0:T(8,128)(2,1)}), (bf16[192,1152]{1,0:T(8,128)(2,1)}, bf16[192,384]{1,0:T(8,128)(2,1)}, ...) | async-done | bytes 1769488 | tf_op jit(solution)/shard_map/psum | solution.py:244
  (194 shorter events, 73.1 us)
Async XLA Ops:
  7.2 112.5 %all-gather.4.cloned.1.call-start = ((), (), s32[]{:S(2)}) async-start(), calls=%async_computation.4 | async-start | bytes 1769472 | tf_op jit(solution)/shard_map/all_gather | solution.py:85
  7.9 138.1 %all-gather.6.cloned.1.call-start = ((), (), s32[]{:S(2)}) async-start(), calls=%async_computation.5 | async-start | bytes 1769472 | tf_op jit(solution)/shard_map/all_gather | solution.py:87
  8.7 250.9 %reduce-scatter.7.cloned.1.call-start = ((), (), s32[]{:S(2)}) async-start(), calls=%async_computation.7 | async-start | bytes 442368 | tf_op jit(solution)/shard_map/reduce_scatter | solution.py:216
  10.4 5.0 %copy-start.32 = (bf16[192]{0:T(256)(128)(2,1)S(1)}, bf16[192]{0:T(256)(128)(2,1)}, u32[]{:S(2)}) copy-start(bf16[192]{0:T(256)(128)(2,1)} %param.20) | copy-start | bytes 1156
  10.4 5.2 %copy-start.33 = (bf16[192]{0:T(256)(128)(2,1)S(1)}, bf16[192]{0:T(256)(128)(2,1)}, u32[]{:S(2)}) copy-start(bf16[192]{0:T(256)(128)(2,1)} %param.22) | copy-start | bytes 1156
  10.4 5.5 %copy-start.34 = (bf16[192]{0:T(256)(128)(2,1)S(1)}, bf16[192]{0:T(256)(128)(2,1)}, u32[]{:S(2)}) copy-start(bf16[192]{0:T(256)(128)(2,1)} %param.23) | copy-start | bytes 1156
  10.4 5.7 %copy-start.35 = (bf16[192]{0:T(256)(128)(2,1)S(1)}, bf16[192]{0:T(256)(128)(2,1)}, u32[]{:S(2)}) copy-start(bf16[192]{0:T(256)(128)(2,1)} %param.24) | copy-start | bytes 1156
  12.3 32.1 %copy-start.19 = (f32[1576]{0:T(1024)}, f32[1576]{0:T(1024)S(1)}, u32[]{:S(2)}) copy-start(f32[1576]{0:T(1024)S(1)} %div.27) | copy-start | bytes 18916
  13.2 31.2 %copy-start.21 = (f32[1576]{0:T(1024)}, f32[1576]{0:T(1024)S(1)}, u32[]{:S(2)}) copy-start(f32[1576]{0:T(1024)S(1)} %rsqrt.21) | copy-start | bytes 18916
  22.3 91.6 %copy-start.23 = (f32[384]{0:T(512)}, f32[384]{0:T(512)S(1)}, u32[]{:S(2)}) copy-start(f32[384]{0:T(512)S(1)} %convert_element_type.205) | copy-start | bytes 4612
  24.4 25.1 %copy-start.4 = (f32[1576,384]{1,0:T(8,128)}, f32[1576,384]{1,0:T(8,128)S(1)}, u32[]{:S(2)}) copy-start(f32[1576,384]{1,0:T(8,128)S(1)} %reshape.179) | copy-start | bytes 7262212
  71.4 5.6 %copy-start.9 = (bf16[8,197,1,6,64]{1,4,3,0,2:T(8,128)(2,1)}, bf16[8,197,1,6,64]{1,4,3,0,2:T(8,128)(2,1)S(1)}, u32[]{:S(2)}) copy-start(bf16[8,197,1,6,64]{1,4,3,0,2:T(8,128)(2,1)S(1)} %copy.114) | copy-start | bytes 3631108
  84.3 6.3 %copy-start.7 = (bf16[8,197,1,6,64]{1,4,3,0,2:T(8,128)(2,1)}, bf16[8,197,1,6,64]{1,4,3,0,2:T(8,128)(2,1)S(1)}, u32[]{:S(2)}) copy-start(bf16[8,197,1,6,64]{1,4,3,0,2:T(8,128)(2,1)S(1)} %copy.113) | copy-start | bytes 3631108
  103.6 51.0 %copy-start.2 = (f32[1576,384]{1,0:T(8,128)}, f32[1576,384]{1,0:T(8,128)S(1)}, u32[]{:S(2)}) copy-start(f32[1576,384]{1,0:T(8,128)S(1)} %get-tuple-element.127) | copy-start | bytes 7262212
  146.0 8.6 %copy-start.28 = (bf16[384,1536]{1,0:T(8,128)(2,1)S(1)}, bf16[384,1536]{1,0:T(8,128)(2,1)}, u32[]{:S(2)}) copy-start(bf16[384,1536]{1,0:T(8,128)(2,1)} %all-gather.4.cloned.1.call-done) | copy-start | bytes 3538948
  197.2 5.2 %copy-start.10 = (bf16[8,197,1,6,64]{1,4,3,0,2:T(8,128)(2,1)S(1)}, bf16[8,197,1,6,64]{1,4,3,0,2:T(8,128)(2,1)}, u32[]{:S(2)}) copy-start(bf16[8,197,1,6,64]{1,4,3,0,2:T(8,128)(2,1)} %copy-done.9) | copy-start | bytes 3631108
  197.2 10.7 %slice-start = ((s8[9830400]{0:T(1024)(128)(4,1)}), s8[4194304]{0:T(1024)(128)(4,1)S(1)}, s32[]{:S(2)}) async-start(s8[9830400]{0:T(1024)(128)(4,1)} %bitcast.70), calls=%async_computation.11 | async-start | bytes 8388608
  197.2 10.7 %slice-start.1 = ((s8[9830400]{0:T(1024)(128)(4,1)}), s8[4194304]{0:T(1024)(128)(4,1)S(1)}, s32[]{:S(2)}) async-start(s8[9830400]{0:T(1024)(128)(4,1)} %bitcast.70), calls=%async_computation.12 | async-start | bytes 8388608
  202.4 5.4 %slice-start.2 = ((s8[9830400]{0:T(1024)(128)(4,1)}), s8[1441792]{0:T(1024)(128)(4,1)S(1)}, s32[]{:S(2)}) async-start(s8[9830400]{0:T(1024)(128)(4,1)} %bitcast.70), calls=%async_computation.13 | async-start | bytes 2883584
  202.4 5.4 %copy-start.8 = (bf16[8,197,6,64]{1,3,2,0:T(8,128)(2,1)S(1)}, bf16[8,197,6,64]{1,3,2,0:T(8,128)(2,1)}, u32[]{:S(2)}) copy-start(bf16[8,197,6,64]{1,3,2,0:T(8,128)(2,1)} %copy.95) | copy-start | bytes 3631108
  211.0 48.6 %reduce-scatter.5.cloned.1.call-start = ((), (), s32[]{:S(2)}) async-start(), calls=%async_computation.6 | async-start | bytes 1327104 | tf_op jit(solution)/shard_map/reduce_scatter | solution.py:207
  233.9 43.2 %reduce-scatter.9.cloned.1.call-start = ((), (), s32[]{:S(2)}) async-start(), calls=%async_computation.8 | async-start | bytes 1769472 | tf_op jit(solution)/shard_map/reduce_scatter | solution.py:228
  240.6 61.0 %reduce-scatter.11.cloned.1.call-start = ((), (), s32[]{:S(2)}) async-start(), calls=%async_computation.9 | async-start | bytes 1769472 | tf_op jit(solution)/shard_map/reduce_scatter | solution.py:234
  240.6 9.8 %copy-start.36 = (bf16[192]{0:T(256)(128)(2,1)S(1)}, bf16[192]{0:T(256)(128)(2,1)}, u32[]{:S(2)}) copy-start(bf16[192]{0:T(256)(128)(2,1)} %param.28) | copy-start | bytes 1156
  240.6 10.3 %copy-start.14 = (bf16[384,1152]{1,0:T(8,128)(2,1)S(1)}, bf16[384,1152]{1,0:T(8,128)(2,1)}, u32[]{:S(2)}) copy-start(bf16[384,1152]{1,0:T(8,128)(2,1)} %copy-done.13) | copy-start | bytes 2654212
  240.7 10.2 %copy-start.20 = (f32[1576]{0:T(1024)S(1)}, f32[1576]{0:T(1024)}, u32[]{:S(2)}) copy-start(f32[1576]{0:T(1024)} %copy-done.19) | copy-start | bytes 18916
  240.7 10.2 %copy-start.22 = (f32[1576]{0:T(1024)S(1)}, f32[1576]{0:T(1024)}, u32[]{:S(2)}) copy-start(f32[1576]{0:T(1024)} %copy-done.21) | copy-start | bytes 18916
  240.7 10.2 %copy-start.24 = (f32[384]{0:T(512)S(1)}, f32[384]{0:T(512)}, u32[]{:S(2)}) copy-start(f32[384]{0:T(512)} %copy-done.23) | copy-start | bytes 4612
  247.5 155.3 %all-reduce.23.cloned.1.call-start = ((), (), s32[]{:S(2)}) async-start(), calls=%async_computation.10 | async-start | bytes 3538944 | tf_op jit(solution)/shard_map/psum | solution.py:244
  250.9 6.5 %copy-start.5 = (f32[1576,384]{1,0:T(8,128)S(1)}, f32[1576,384]{1,0:T(8,128)}, u32[]{:S(2)}) copy-start(f32[1576,384]{1,0:T(8,128)} %copy-done.4) | copy-start | bytes 7262212
  347.0 5.5 %copy-start.3 = (f32[1576,384]{1,0:T(8,128)S(1)}, f32[1576,384]{1,0:T(8,128)}, u32[]{:S(2)}) copy-start(f32[1576,384]{1,0:T(8,128)} %copy-done.2) | copy-start | bytes 7262212
  402.8 5.4 %copy-start.18 = (bf16[192,384]{1,0:T(8,128)(2,1)S(1)}, bf16[192,384]{1,0:T(8,128)(2,1)}, u32[]{:S(2)}) copy-start(bf16[192,384]{1,0:T(8,128)(2,1)} %get-tuple-element.93) | copy-start | bytes 442372
  (16 other events, 48.3 us)
Sparse Core Ops, SparseCore 0:
  9.6 32.8 all-gather.3
  44.0 22.3 all-gather.5
  211.1 12.0 reduce-scatter.6
  234.0 18.5 reduce-scatter.4
  255.3 21.7 reduce-scatter.8
  279.8 21.7 reduce-scatter.10
  305.5 97.2 all-reduce.22
where the time goes:
time: 421 us; the launch traced here: 416 us
  matrix products  113 us (27%)
  local copies, waits for them, and re-layouts  85.2 us (20%)
  waiting for transfers between devices  84.9 us (20%)
  blocking collectives  75.7 us (18%)
  other arithmetic  39.7 us (9%)
  between operations  17 us (4%)
    psum x1, waiting for transfers between devices, per_device(): lax.psum(owned[2].astype(jnp.bfloat16), 'rep').astype(jnp.float32)  41.4 us
    dot_general x4, matrix products, product(): return jnp.dot(left, right, preferred_element_type=jnp.float32)  39.9 us
    psum x1, blocking collectives, per_device(): lax.psum(owned[0].astype(jnp.bfloat16), 'rep').astype(jnp.float32)  32.4 us
    reduce_scatter x1, waiting for transfers between devices, per_device(): lax.psum_scatter(grad_drop_weight.astype(jnp.bfloat16), 'fsdp', scatter_d...  24.5 us
    unnamed x116, local copies, waits for them, and re-layouts  23.6 us
    dot_general x4, matrix products, product_left(): lax.dot_general(left, right, (((0,), (0,)), ((), ())), preferred_element_...  20.4 us
    dot_general x4, matrix products, product_right(): lax.dot_general(left, right, (((1,), (1,)), ((), ())), preferred_element_...  20.3 us
    all_gather x1, blocking collectives, per_device(): lax.all_gather(qkv_weight, 'fsdp', axis=0, tiled=True)  20 us
  transfers between devices with their start and end apart: 7, of which 3 were waited for; matrix products, arithmetic and copies ran while one was open for 39% of the time, Pallas kernels for 0%

commit v1 on v0

--- a/solution.py
+++ b/solution.py
@@ -8,6 +8,18 @@
 epsilon = 1e-06
 root_half = 0.7071067811865476
 gauss_norm = 0.3989422804014327
+
+
+def gather_by_bits(x, axis, dim):
+    ways, here, step = (lax.axis_size(axis), lax.axis_index(axis), x.shape[dim])
+    line, have = (x, 1)
+    while have < ways:
+        line = jnp.concatenate(
+            [line, lax.ppermute(line, axis, [(d, (d - have) % ways) for d in range(ways)])],
+            axis=dim,
+        )
+        have = 2 * have
+    return jnp.roll(line, here * step, axis=dim)
 
 
 def norm_forward(inputs, gain_vec, shift_vec):
@@ -75,7 +87,7 @@
     gathered = (
         lax.all_gather(gain_one, "fsdp", axis=0, tiled=True),
         lax.all_gather(shift_one, "fsdp", axis=0, tiled=True),
-        lax.all_gather(qkv_weight, "fsdp", axis=0, tiled=True),
+        gather_by_bits(qkv_weight, "fsdp", 0),
         lax.all_gather(query_bias, "fsdp", axis=0, tiled=True),
         lax.all_gather(value_bias, "fsdp", axis=0, tiled=True),
         lax.all_gather(out_weight, "fsdp", axis=0, tiled=True),

time: 421 us -> 407 us (0.967)
  waiting for transfers between devices: 84.9 us -> 74.6 us
  blocking collectives: 75.7 us -> 65.5 us
    reduce_scatter x1, waiting for transfers between devices: 17.5 us -> 7.81 us  [per_device(): lax.psum_scatter(grad_lift_weight.astype(jnp.bfloat16), 'fsdp', scatter_d...]
    all_gather x1, blocking collectives: 20 us -> 11 us  [per_device(): lax.all_gather(qkv_weight, 'fsdp', axis=0, tiled=True)]
    unnamed x116 -> x114, local copies, waits for them, and re-layouts: 23.6 us -> 22.3 us
  transfers between devices with their start and end apart: 7 -> 8, of which waited for: 3 -> 3; matrix products, arithmetic and copies ran while one was open for 39% -> 42% of each run, Pallas kernels for 0% -> 0%
where the time goes in v1:
time: 407 us; the launch traced here: 401 us
  matrix products  116 us (29%)
  local copies, waits for them, and re-layouts  83.8 us (21%)
  waiting for transfers between devices  74.6 us (18%)
  blocking collectives  65.5 us (16%)
  other arithmetic  40 us (10%)
  between operations  17.3 us (4%)
    dot_general x4, matrix products, product(): return jnp.dot(left, right, preferred_element_type=jnp.float32)  42.8 us
    psum x1, waiting for transfers between devices, per_device(): lax.psum(owned[2].astype(jnp.bfloat16), 'rep').astype(jnp.float32)  41.4 us
    psum x1, blocking collectives, per_device(): lax.psum(owned[0].astype(jnp.bfloat16), 'rep').astype(jnp.float32)  32.4 us
    reduce_scatter x1, waiting for transfers between devices, per_device(): lax.psum_scatter(grad_drop_weight.astype(jnp.bfloat16), 'fsdp', scatter_d...  24.6 us
    unnamed x114, local copies, waits for them, and re-layouts  22.3 us
    dot_general x4, matrix products, product_right(): lax.dot_general(left, right, (((1,), (1,)), ((), ())), preferred_element_...  20.6 us
    dot_general x4, matrix products, product_left(): lax.dot_general(left, right, (((0,), (0,)), ((), ())), preferred_element_...  20.3 us
    convert_element_type x2, local copies, waits for them, and re-layouts, per_device(): d_projected = jnp.stack([d_query, d_key, d_value], axis=2).reshape(tok_ro...  14.3 us
  transfers between devices with their start and end apart: 8, of which 3 were waited for; matrix products, arithmetic and copies ran while one was open for 42% of the time, Pallas kernels for 0%

profile of v1, /device:TPU:0, one launch (start us, length us, event | category | flops | bytes accessed | tf_op | source)
XLA Modules:
  0.0 400.8 jit_solution(16456336239138708433)
XLA Ops:
  18.7 5.0 %all-reduce.20 = (bf16[384]{0:T(512)(128)(2,1)S(1)}, bf16[384]{0:T(512)(128)(2,1)S(1)}, bf16[384]{0:T(512)(128)(2,1)S(1)}, bf16[384]{0:T(512)(128)(2,1)S(1)}, bf...) all-reduce(bf16[384]{0:T(512)(128)(2,1)S(1)} %dynamic-update-slice., ...), channel_id=1, replica_groups=mesh['rep'=16,'fsdp'=2] {'fsdp'}, use_global_device_ids=true, to_apply=%add.3 | all-reduce | flops 2688 | bytes 10752
  25.8 4.4 %all-gather = bf16[2,1,768]{2,1,0:T(2,128)(2,1)S(1)} all-gather(bf16[1,1,768]{2,1,0:T(2,128)(2,1)S(1)} %reshape.209), channel_id=1, replica_groups=mesh['rep'=16,'fsdp'=2] {'fsdp'}, dimensions={0}, use_global_device_ids=true | all-gather | bytes 4608 | tf_op jit(solution)/shard_map/all_gather | solution.py:98
  41.1 5.8 %all_gather.48 = bf16[384,384]{1,0:T(8,128)(2,1)S(1)} all-gather(bf16[192,384]{1,0:T(8,128)(2,1)S(1)} %copy-done.16), channel_id=1, replica_groups=mesh['rep'=16,'fsdp'=2] {'fsdp'}, dimensions={0}, use_global_device_ids=true | all-gather | bytes 442368 | tf_op jit(solution)/shard_map/all_gather | solution.py:93
  47.0 6.9 %fusion.16 = bf16[1576,1152]{1,0:T(8,128)(2,1)} fusion(f32[1152]{0:T(1024)S(1)} %maximum_convert_fusion.1, f32[1576,384]{1,0:T(8,128)S(1)} %reshape.179, f32[384]{0:T(512)S(1)} %convert_element_type.206, f32[384]{0:T(512)S(1)} %convert_element_type.205, f32[1576]{0:T(1024)S(1)} %rsqrt.21, f32[1576]{0:T(1024)S(1)} %div.27, s32[]{:T(128)S(6)} %select_n.14, ...), kind=kOutput, calls=%fused_computation.34 | convolution fusion | flops 1404539904 | bytes 6956868 | tf_op jit(solution)/shard_map/dot_general | solution.py:47
  53.9 11.7 %reshape.237 = bf16[8,197,3,6,64]{4,3,2,1,0:T(8,128)(2,1)} reshape(bf16[1576,1152]{1,0:T(8,128)(2,1)} %fusion.16) | data formatting | bytes 7262208 | tf_op jit(solution)/shard_map/reshape | solution.py:129
  65.6 6.7 %fusion.49 = (bf16[8,197,1,6,64]{4,3,2,1,0:T(8,128)(2,1)}, bf16[8,197,1,6,64]{4,3,2,1,0:T(8,128)(2,1)}, bf16[8,197,1,6,64]{4,3,2,1,0:T(8,128)(2,1)}) fusion(bf16[8,197,3,6,64]{4,3,2,1,0:T(8,128)(2,1)} %reshape.237), kind=kLoop, calls=%fused_computation.105 | loop fusion | bytes 7262208 | tf_op jit(solution)/shard_map/slice | solution.py:130
  72.3 3.5 copy.114
  75.8 4.0 %copy.115 = bf16[8,197,1,6,64]{1,4,3,0,2:T(8,128)(2,1)S(1)} copy(bf16[8,197,1,6,64]{4,3,2,1,0:T(8,128)(2,1)} %get-tuple-element.119) | data formatting | bytes 2420736
  85.2 3.5 copy.113
  88.7 6.3 %fusion.29 = bf16[8,197,6,64]{1,3,2,0:T(8,128)(2,1)S(1)} fusion(bf16[8,197,1,6,64]{1,4,3,0,2:T(8,128)(2,1)S(1)} %copy.113, f32[8,6,197,197]{2,3,1,0:T(8,128)} %copy-done, f32[8,6,197]{2,1,0:T(8,128)S(1)} %log_add_fusion), kind=kOutput, calls=%fused_computation.77 | convolution fusion | flops 244636176 | bytes 9909888 | tf_op jit(solution)/shard_map/ihqk,ikhe->iqhe/dot_general | solution.py:138
  102.8 26.6 %fusion.2 = (bf16[1576,1536]{1,0:T(8,128)(2,1)}, f32[1576,1536]{1,0:T(8,128)}) fusion(f32[1536]{0:T(1024)S(1)} %reshape.211, bf16[384,1536]{1,0:T(8,128)(2,1)} %all-gather.4.cloned.1.call-done, f32[1576,384]{1,0:T(8,128)S(1)} %get-tuple-element.127, f32[384]{0:T(512)S(1)} %convert_element_type.216, f32[384]{0:T(512)S(1)} %convert_element_type.215, ...), kind=kOutput, calls=%fused_computation.9 | convolution fusion | flops 2021919744 | bytes 18146624 | tf_op jit(solution)/shard_map/dot_general | solution.py:47
  129.4 8.6 %fusion.53 = (bf16[1536]{0:T(1024)(128)(2,1)S(1)}, bf16[1576,1536]{1,0:T(8,128)(2,1)S(1)}) fusion(f32[1576,1536]{1,0:T(8,128)} %get-tuple-element.129, bf16[1576,384]{1,0:T(8,128)(2,1)} %reshape.182, bf16[1536,384]{1,0:T(8,128)(2,1)} %all-gather.6.cloned.1.call-done), kind=kOutput, calls=%fused_computation.109 | convolution fusion | flops 1885751808 | bytes 16917504 | tf_op jit(solution)/shard_map/dot_general | solution.py:57
  141.3 3.4 convert_reduce_fusion.2
  148.4 4.8 %reshape.238 = bf16[8,197,6,64]{3,2,1,0:T(8,128)(2,1)} reshape(bf16[1576,384]{1,0:T(8,128)(2,1)} %convolution_convert_fusion.3) | data formatting | bytes 2420736 | tf_op jit(solution)/shard_map/reshape | solution.py:182
  153.1 4.6 %copy.95 = bf16[8,197,6,64]{1,3,2,0:T(8,128)(2,1)} copy(bf16[8,197,6,64]{3,2,1,0:T(8,128)(2,1)} %reshape.238) | data formatting | bytes 2420736 | tf_op jit(solution)/shard_map/reshape | solution.py:182
  157.7 11.1 %multiply_reduce_fusion = (f32[8,6,197]{2,1,0:T(8,128)S(1)}, f32[8,6,197,197]{2,3,1,0:T(8,128)}) fusion(f32[8,6,197,197]{2,3,1,0:T(8,128)} %copy-done, f32[8,6,197]{2,1,0:T(8,128)S(1)} %log_add_fusion, bf16[8,197,6,64]{1,3,2,0:T(8,128)(2,1)} %copy.95, bf16[8,197,1,6,64]{1,4,3,0,2:T(8,128)(2,1)} %copy-done.7), kind=kOutput, calls=%fused_computation.3 | convolution fusion | flops 245884368 | bytes 17399040 | tf_op jit(solution)/shard_map/iqhe,ikhe->ihqk/dot_general | solution.py:187
  168.8 11.5 %multiply_convert_fusion = bf16[8,6,197,197]{2,3,1,0:T(8,128)(2,1)} fusion(f32[8,6,197,197]{2,3,1,0:T(8,128)} %get-tuple-element.132, f32[8,6,197,197]{2,3,1,0:T(8,128)} %copy-done, f32[8,6,197]{2,1,0:T(8,128)S(1)} %get-tuple-element.131, f32[8,6,197]{2,1,0:T(8,128)S(1)} %log_add_fusion), kind=kLoop, calls=%fused_computation.2 | loop fusion | flops 9314160 | bytes 18703968 | tf_op jit(solution)/shard_map/convert_element_type | solution.py:189
  180.3 5.2 %multiply_bitcast_fusion.1 = bf16[8,197,1,6,64]{1,4,3,0,2:T(8,128)(2,1)} fusion(bf16[8,6,197,197]{2,3,1,0:T(8,128)(2,1)} %multiply_convert_fusion, bf16[8,197,1,6,64]{1,4,3,0,2:T(8,128)(2,1)} %copy-done.1), kind=kOutput, calls=%fused_computation.37 | convolution fusion | flops 239652864 | bytes 6146400 | tf_op jit(solution)/shard_map/ihqk,ikhe->iqhe/dot_general | solution.py:191
  185.5 5.4 %multiply_bitcast_fusion = bf16[8,197,1,6,64]{1,4,3,0,2:T(8,128)(2,1)} fusion(bf16[8,6,197,197]{2,3,1,0:T(8,128)(2,1)} %multiply_convert_fusion, bf16[8,197,1,6,64]{1,4,3,0,2:T(8,128)(2,1)S(1)} %copy-done.10), kind=kOutput, calls=%fused_computation.36 | convolution fusion | flops 239652864 | bytes 6146400 | tf_op jit(solution)/shard_map/ihqk,iqhe->ikhe/dot_general | solution.py:195
  197.4 5.5 %copy.100 = bf16[8,197,3,6,64]{1,0,4,3,2:T(8,128)(2,1)} copy(bf16[8,197,3,6,64]{1,4,3,0,2:T(8,128)(2,1)S(1)} %get-tuple-element.116) | data formatting | bytes 7262208 | tf_op jit(solution)/shard_map/convert_element_type | solution.py:201
  202.8 8.9 %convert_element_type.228 = bf16[1576,1152]{0,1:T(8,128)(2,1)} reshape(bf16[8,197,3,6,64]{1,0,4,3,2:T(8,128)(2,1)} %copy.100) | data formatting | bytes 7262208 | tf_op jit(solution)/shard_map/convert_element_type | solution.py:201
  211.7 5.3 %convolution_convert_fusion = bf16[384,1152]{1,0:T(8,128)(2,1)} fusion(bf16[1576,384]{1,0:T(8,128)(2,1)} %convert_element_type.235, bf16[1576,1152]{0,1:T(8,128)(2,1)} %convert_element_type.228), kind=kOutput, calls=%fused_computation.42 | convolution fusion | flops 1394786304 | bytes 5726208 | tf_op jit(solution)/shard_map/dot_general | solution.py:51
  217.1 6.6 %convolution_convert_fusion.2 = bf16[384,1536]{1,0:T(8,128)(2,1)} fusion(bf16[1576,1536]{1,0:T(8,128)(2,1)} %copy-done.36, f32[1576,384]{1,0:T(8,128)} %copy-done.2, f32[384]{0:T(512)S(1)} %convert_element_type.216, f32[384]{0:T(512)S(1)} %convert_element_type.215, f32[1576]{0:T(1024)S(1)} %add_rsqrt_fusion, f32[1576]{0:T(1024)S(1)} %broadcast_multiply_fusion.4), kind=kOutput, calls=%fused_computation.45 | convolution fusion | flops 1862740992 | bytes 8457536 | tf_op jit(solution)/shard_map/dot_general | solution.py:51
  223.8 6.7 %convolution_convert_fusion.1 = bf16[1536,384]{1,0:T(8,128)(2,1)} fusion(bf16[1576,1536]{1,0:T(8,128)(2,1)} %get-tuple-element.128, bf16[1576,384]{1,0:T(8,128)(2,1)} %reshape.182), kind=kOutput, calls=%fused_computation.44 | convolution fusion | flops 1859715072 | bytes 7231488 | tf_op jit(solution)/shard_map/dot_general | solution.py:51
  233.8 11.0 %all_gather.56 = bf16[384,1152]{1,0:T(8,128)(2,1)S(1)} all-gather(bf16[192,1152]{1,0:T(8,128)(2,1)S(1)} %copy-done.14), channel_id=1, replica_groups=mesh['rep'=16,'fsdp'=2] {'fsdp'}, dimensions={0}, use_global_device_ids=true | all-gather | bytes 1327104 | tf_op jit(solution)/shard_map/all_gather | solution.py:153
  244.8 6.7 %multiply_reduce_fusion.3 = (bf16[384]{0:T(512)(128)(2,1)S(1)}, f32[1576]{0:T(1024)S(1)}, f32[1576]{0:T(1024)S(1)}, bf16[384]{0:T(512)(128)(2,1)S(1)}, f32[1576,384]{1,0:T(8,128)S(1)}) fusion(f32[1576,384]{1,0:T(8,128)} %copy-done.4, f32[1576]{0:T(1024)S(1)} %copy-done.21, f32[1576]{0:T(1024)S(1)} %copy-done.19, f32[384]{0:T(512)S(1)} %copy-done.23, ...), kind=kOutput, calls=%fused_computation.49 | convolution fusion | flops 1399786752 | bytes 9385600 | tf_op jit(solution)/shard_map/dot_general | solution.py:57
  253.8 7.8 %reduce-scatter.9.cloned.1.call-done = bf16[192,1536]{1,0:T(8,128)(2,1)} async-done(((bf16[384,1536]{1,0:T(8,128)(2,1)}), bf16[192,1536]{1,0:T(8,128)(2,1)}) %reduce-scatter.9.cloned.1.call-update) | async-done | bytes 589840 | tf_op jit(solution)/shard_map/reduce_scatter | solution.py:240
  261.6 24.6 %reduce-scatter.11.cloned.1.call-done = bf16[768,384]{1,0:T(8,128)(2,1)} async-done(((bf16[1536,384]{1,0:T(8,128)(2,1)}), bf16[768,384]{1,0:T(8,128)(2,1)}) %reduce-scatter.11.cloned.1.call-update) | async-done | bytes 589840 | tf_op jit(solution)/shard_map/reduce_scatter | solution.py:246
  286.4 7.0 %all-reduce.19 = (bf16[384]{0:T(512)(128)(2,1)S(1)}, bf16[384]{0:T(512)(128)(2,1)S(1)}, bf16[384]{0:T(512)(128)(2,1)S(1)}, bf16[384]{0:T(512)(128)(2,1)S(1)}, bf...) all-reduce(bf16[384]{0:T(512)(128)(2,1)S(1)} %dynamic-update-slice., ...), channel_id=1, replica_groups=mesh['rep'=16,'fsdp'=2] {'fsdp'}, use_global_device_ids=true, to_apply=%add.7 | all-reduce | flops 4992 | bytes 19968
  294.0 32.4 %all-reduce.17 = (bf16[192]{0:T(256)(128)(2,1)S(1)}, bf16[192]{0:T(256)(128)(2,1)S(1)}, bf16[192]{0:T(256)(128)(2,1)S(1)}, bf16[192]{0:T(256)(128)(2,1)S(1)}, bf...) all-reduce(bf16[192]{0:T(256)(128)(2,1)S(1)} %dynamic-slice.9, ...), channel_id=1, replica_groups=mesh['rep'=16,'fsdp'=2] {'rep'}, use_global_device_ids=true, to_apply=%region_13.14 | all-reduce | flops 2304 | bytes 9216 | tf_op jit(solution)/shard_map/psum | solution.py:254
  337.0 6.1 %fusion.20 = bf16[1576,384]{1,0:T(8,128)(2,1)} fusion(f32[1576,384]{1,0:T(8,128)S(1)} %copy-done.3, bf16[1576,1536]{1,0:T(8,128)(2,1)} %get-tuple-element.128, bf16[1536,384]{1,0:T(8,128)(2,1)S(1)} %copy-done.26, f32[384]{0:T(512)S(1)} %convert_element_type.220), kind=kOutput, calls=%fused_computation.43 | convolution fusion | flops 1860940800 | bytes 9653760 | tf_op jit(solution)/shard_map/dot_general | solution.py:47
  345.9 41.4 %all-reduce.23.cloned.1.call-done = (bf16[192,1152]{1,0:T(8,128)(2,1)}, bf16[192,384]{1,0:T(8,128)(2,1)}, bf16[192,1536]{1,0:T(8,128)(2,1)}, bf16[768,384]{1,0:T(8,128)(2,1)}) async-done(((bf16[192,1152]{1,0:T(8,128)(2,1)}, bf16[192,384]{1,0:T(8,128)(2,1)}, bf16[192,1536]{1,0:T(8,128)(2,1)}, bf16[768,384]{1,0:T(8,128)(2,1)}), (bf16[192,1152]{1,0:T(8,128)(2,1)}, bf16[192,384]{1,0:T(8,128)(2,1)}, ...) | async-done | bytes 1769488 | tf_op jit(solution)/shard_map/psum | solution.py:256
  (194 shorter events, 74.6 us)
Async XLA Ops:
  7.2 5.5 %copy-start.6 = (bf16[8,197,384]{2,0,1:T(8,128)(2,1)S(1)}, bf16[8,197,384]{2,0,1:T(8,128)(2,1)}, u32[]{:S(2)}) copy-start(bf16[8,197,384]{2,0,1:T(8,128)(2,1)} %param.15) | copy-start | bytes 3631108
  7.2 95.6 %all-gather.4.cloned.1.call-start = ((), (), s32[]{:S(2)}) async-start(), calls=%async_computation.4 | async-start | bytes 1769472 | tf_op jit(solution)/shard_map/all_gather | solution.py:97
  7.9 121.4 %all-gather.6.cloned.1.call-start = ((), (), s32[]{:S(2)}) async-start(), calls=%async_computation.5 | async-start | bytes 1769472 | tf_op jit(solution)/shard_map/all_gather | solution.py:99
  8.0 39.0 %collective-permute-start = (bf16[192,1152]{1,0:T(8,128)(2,1)}, bf16[192,1152]{1,0:T(8,128)(2,1)}, u32[]{:S(2)}, u32[]{:S(2)}) collective-permute-start(bf16[192,1152]{1,0:T(8,128)(2,1)} %param.18), channel_id=1, source_target_pairs={{0,1},{1,0},{2,3},{3,2},{4,5},{5,4},{6,7},{7,6},{8,9},{9,8},{10,11... | collective-permute-start | bytes 1327112 | tf_op jit(solution)/shard_map/ppermute | solution.py:18
  11.0 242.8 %reduce-scatter.7.cloned.1.call-start = ((), (), s32[]{:S(2)}) async-start(), calls=%async_computation.7 | async-start | bytes 442368 | tf_op jit(solution)/shard_map/reduce_scatter | solution.py:228
  12.7 5.3 %copy-start.32 = (bf16[192]{0:T(256)(128)(2,1)S(1)}, bf16[192]{0:T(256)(128)(2,1)}, u32[]{:S(2)}) copy-start(bf16[192]{0:T(256)(128)(2,1)} %param.22) | copy-start | bytes 1156
  12.7 5.5 %copy-start.33 = (bf16[192]{0:T(256)(128)(2,1)S(1)}, bf16[192]{0:T(256)(128)(2,1)}, u32[]{:S(2)}) copy-start(bf16[192]{0:T(256)(128)(2,1)} %param.23) | copy-start | bytes 1156
  12.7 5.7 %copy-start.34 = (bf16[192]{0:T(256)(128)(2,1)S(1)}, bf16[192]{0:T(256)(128)(2,1)}, u32[]{:S(2)}) copy-start(bf16[192]{0:T(256)(128)(2,1)} %param.24) | copy-start | bytes 1156
  14.7 32.3 %copy-start.18 = (f32[1576]{0:T(1024)}, f32[1576]{0:T(1024)S(1)}, u32[]{:S(2)}) copy-start(f32[1576]{0:T(1024)S(1)} %div.27) | copy-start | bytes 18916
  15.6 31.4 %copy-start.20 = (f32[1576]{0:T(1024)}, f32[1576]{0:T(1024)S(1)}, u32[]{:S(2)}) copy-start(f32[1576]{0:T(1024)S(1)} %rsqrt.21) | copy-start | bytes 18916
  23.7 23.3 %copy-start.22 = (f32[384]{0:T(512)}, f32[384]{0:T(512)S(1)}, u32[]{:S(2)}) copy-start(f32[384]{0:T(512)S(1)} %convert_element_type.205) | copy-start | bytes 4612
  25.8 21.3 %copy-start.4 = (f32[1576,384]{1,0:T(8,128)}, f32[1576,384]{1,0:T(8,128)S(1)}, u32[]{:S(2)}) copy-start(f32[1576,384]{1,0:T(8,128)S(1)} %reshape.179) | copy-start | bytes 7262212
  37.2 9.8 %copy-start.13 = (bf16[192,1152]{1,0:T(8,128)(2,1)S(1)}, bf16[192,1152]{1,0:T(8,128)(2,1)}, u32[]{:S(2)}) copy-start(bf16[192,1152]{1,0:T(8,128)(2,1)} %param.18) | copy-start | bytes 1327108
  75.8 5.6 %copy-start.9 = (bf16[8,197,1,6,64]{1,4,3,0,2:T(8,128)(2,1)}, bf16[8,197,1,6,64]{1,4,3,0,2:T(8,128)(2,1)S(1)}, u32[]{:S(2)}) copy-start(bf16[8,197,1,6,64]{1,4,3,0,2:T(8,128)(2,1)S(1)} %copy.114) | copy-start | bytes 3631108
  88.7 6.3 %copy-start.7 = (bf16[8,197,1,6,64]{1,4,3,0,2:T(8,128)(2,1)}, bf16[8,197,1,6,64]{1,4,3,0,2:T(8,128)(2,1)S(1)}, u32[]{:S(2)}) copy-start(bf16[8,197,1,6,64]{1,4,3,0,2:T(8,128)(2,1)S(1)} %copy.113) | copy-start | bytes 3631108
  102.2 35.8 %copy-start.2 = (f32[1576,384]{1,0:T(8,128)}, f32[1576,384]{1,0:T(8,128)S(1)}, u32[]{:S(2)}) copy-start(f32[1576,384]{1,0:T(8,128)S(1)} %get-tuple-element.127) | copy-start | bytes 7262212
  129.4 8.6 %copy-start.27 = (bf16[384,1536]{1,0:T(8,128)(2,1)S(1)}, bf16[384,1536]{1,0:T(8,128)(2,1)}, u32[]{:S(2)}) copy-start(bf16[384,1536]{1,0:T(8,128)(2,1)} %all-gather.4.cloned.1.call-done) | copy-start | bytes 3538948
  180.3 10.7 %slice-start = ((s8[9830400]{0:T(1024)(128)(4,1)}), s8[4194304]{0:T(1024)(128)(4,1)S(1)}, s32[]{:S(2)}) async-start(s8[9830400]{0:T(1024)(128)(4,1)} %bitcast.69), calls=%async_computation.11 | async-start | bytes 8388608
  180.3 10.7 %slice-start.1 = ((s8[9830400]{0:T(1024)(128)(4,1)}), s8[4194304]{0:T(1024)(128)(4,1)S(1)}, s32[]{:S(2)}) async-start(s8[9830400]{0:T(1024)(128)(4,1)} %bitcast.69), calls=%async_computation.12 | async-start | bytes 8388608
  185.5 5.4 %slice-start.2 = ((s8[9830400]{0:T(1024)(128)(4,1)}), s8[1441792]{0:T(1024)(128)(4,1)S(1)}, s32[]{:S(2)}) async-start(s8[9830400]{0:T(1024)(128)(4,1)} %bitcast.69), calls=%async_computation.13 | async-start | bytes 2883584
  185.5 5.4 %copy-start.8 = (bf16[8,197,6,64]{1,3,2,0:T(8,128)(2,1)S(1)}, bf16[8,197,6,64]{1,3,2,0:T(8,128)(2,1)}, u32[]{:S(2)}) copy-start(bf16[8,197,6,64]{1,3,2,0:T(8,128)(2,1)} %copy.95) | copy-start | bytes 3631108
  194.1 59.7 %reduce-scatter.5.cloned.1.call-start = ((), (), s32[]{:S(2)}) async-start(), calls=%async_computation.6 | async-start | bytes 1327104 | tf_op jit(solution)/shard_map/reduce_scatter | solution.py:219
  217.0 44.5 %reduce-scatter.9.cloned.1.call-start = ((), (), s32[]{:S(2)}) async-start(), calls=%async_computation.8 | async-start | bytes 1769472 | tf_op jit(solution)/shard_map/reduce_scatter | solution.py:240
  223.7 62.4 %reduce-scatter.11.cloned.1.call-start = ((), (), s32[]{:S(2)}) async-start(), calls=%async_computation.9 | async-start | bytes 1769472 | tf_op jit(solution)/shard_map/reduce_scatter | solution.py:246
  223.8 9.8 %copy-start.35 = (bf16[192]{0:T(256)(128)(2,1)S(1)}, bf16[192]{0:T(256)(128)(2,1)}, u32[]{:S(2)}) copy-start(bf16[192]{0:T(256)(128)(2,1)} %param.28) | copy-start | bytes 1156
  230.5 14.3 %copy-start.19 = (f32[1576]{0:T(1024)S(1)}, f32[1576]{0:T(1024)}, u32[]{:S(2)}) copy-start(f32[1576]{0:T(1024)} %copy-done.18) | copy-start | bytes 18916
  230.5 14.3 %copy-start.21 = (f32[1576]{0:T(1024)S(1)}, f32[1576]{0:T(1024)}, u32[]{:S(2)}) copy-start(f32[1576]{0:T(1024)} %copy-done.20) | copy-start | bytes 18916
  230.5 14.3 %copy-start.23 = (f32[384]{0:T(512)S(1)}, f32[384]{0:T(512)}, u32[]{:S(2)}) copy-start(f32[384]{0:T(512)} %copy-done.22) | copy-start | bytes 4612
  230.6 156.8 %all-reduce.23.cloned.1.call-start = ((), (), s32[]{:S(2)}) async-start(), calls=%async_computation.10 | async-start | bytes 3538944 | tf_op jit(solution)/shard_map/psum | solution.py:256
  244.8 6.8 %copy-start.5 = (f32[1576,384]{1,0:T(8,128)S(1)}, f32[1576,384]{1,0:T(8,128)}, u32[]{:S(2)}) copy-start(f32[1576,384]{1,0:T(8,128)} %copy-done.4) | copy-start | bytes 7262212
  331.5 5.5 %copy-start.3 = (f32[1576,384]{1,0:T(8,128)S(1)}, f32[1576,384]{1,0:T(8,128)}, u32[]{:S(2)}) copy-start(f32[1576,384]{1,0:T(8,128)} %copy-done.2) | copy-start | bytes 7262212
  387.3 5.4 %copy-start.17 = (bf16[192,384]{1,0:T(8,128)(2,1)S(1)}, bf16[192,384]{1,0:T(8,128)(2,1)}, u32[]{:S(2)}) copy-start(bf16[192,384]{1,0:T(8,128)(2,1)} %get-tuple-element.93) | copy-start | bytes 442372
  (16 other events, 58.6 us)
Sparse Core Ops, SparseCore 0:
  9.6 25.6 all-gather.3
  36.9 23.4 all-gather.5
  194.2 12.7 reduce-scatter.6
  217.2 20.0 reduce-scatter.4
  240.0 21.5 reduce-scatter.8
  264.3 21.7 reduce-scatter.10
  290.1 97.2 all-reduce.22
